TPU v7x, 32 devices: a whole 2x2x4 slice. The times are simulated.
32 devices in a mesh: mesh: 8 (over z, core), src: 4 (over y, x).
Axes of the slice: x: 2, y: 2, z: 4, core: 2. Of those that a mesh axis runs over, the one named last changes fastest.
Arguments:
- solution: float32 [512, 24576], P('src', 'mesh'), may hold values from -6 to 6
- conduct: float32 [24576], P('mesh'), may hold values from 0.5 to 2
- source_edge: int32 [512], P('src'), may hold values from 0 to 24575
- source_amp: float32 [512], P('src'), may hold values from -8 to 8
- interior: int32 [8192], P('mesh'), may hold values 0 or 1
- edge_dir: float32 [3, 24576], P(None, 'mesh'), may hold values from -4 to 4
- tail_node: int32 [24576], P('mesh'), may hold values from 0 to 127, as said below
- head_node: int32 [24576], P('mesh'), may hold values from 0 to 383, as said below
- block_inv: float32 [256, 128, 128], P(('mesh', 'src')), may hold values from -1 to 1
- block_op: float32 [256, 128, 128], P(('mesh', 'src')), may hold values from -1 to 4
Outputs:
- correction: float32 [512, 24576], P('src', 'mesh')
Inputs may be any that keep to these rules, and one draw needn't show every extreme that they name: `tail_node`: every value occurs. An edge of block k has head_node of (2 - k) * 128 or more; head_node never equals 256 + tail_node.
All inputs are finite; a program needn't handle non-finite values. No bound on the sum of `interior` on one device may be relied on, other than what follows from the above.
Results may differ from a plain program's by a relative error of at most 0.0034.
Values may be sent and summed in bfloat16 or wider, within the bound.
No kernel may reach another device: no remote copies, remote signals or barrier semaphores. Data moves between devices by JAX's collectives and lax.ppermute only.
A program may use at most 64 MiB of HBM per device.

v0:
```python
import jax
import jax.numpy as jnp
from jax import lax
from jax.sharding import PartitionSpec as P

BLOCK_NODES = 128
TILES_BLOCK = 3
HIGHEST_PREC = lax.Precision.HIGHEST


def shifted(x, axis, by):
    peers = lax.axis_size(axis)
    pairs = [(i, i + by) for i in range(peers) if 0 <= i + by < peers]
    return lax.ppermute(x, axis, pairs)


def spread_heads(head_part, bnodes):
    row_count = head_part.shape[0]
    running = jnp.zeros((row_count + 2,) + head_part.shape[1:3] + (bnodes,), jnp.float32)
    for offset in range(3):
        slab_part = head_part[..., offset * bnodes : (offset + 1) * bnodes]
        running = running + jnp.pad(slab_part, ((offset, 2 - offset), (0, 0), (0, 0), (0, 0)))
    return running


def endpoint_coefs(directions, nblocks, edge_span):
    half_dir = 0.5 * directions.reshape(3, nblocks, edge_span)
    unit_row = jnp.ones((1, nblocks, edge_span), jnp.float32)
    return (jnp.concatenate([-unit_row, half_dir], 0), jnp.concatenate([unit_row, half_dir], 0))


def block_sweep(nodal_rhs, inverse, operator):
    rhs_full = nodal_rhs.astype(jnp.float32)
    first_pass = jnp.einsum("ism,inm->isn", rhs_full, inverse, precision=HIGHEST_PREC)
    defect = rhs_full - jnp.einsum("ism,inm->isn", first_pass, operator, precision=HIGHEST_PREC)
    solved = first_pass + jnp.einsum("ism,inm->isn", defect, inverse, precision=HIGHEST_PREC)
    return solved.astype(jnp.bfloat16)


def shards(
    solution,
    conduct,
    source_edge,
    source_amp,
    interior,
    edge_dir,
    tail_node,
    head_node,
    block_inv,
    block_op,
):
    src_dev, edge_dev = solution.shape
    bnodes = BLOCK_NODES
    edge_span = TILES_BLOCK * bnodes
    nblocks = edge_dev // edge_span
    first_edge = lax.axis_index("mesh") * edge_dev
    edge_ids = first_edge + lax.iota(jnp.int32, edge_dev)
    source_hit = source_edge[:, None] == edge_ids[None, :]
    residual = jnp.where(source_hit, source_amp[:, None], 0.0) - conduct[None, :] * solution
    resid_blocks = residual.reshape(src_dev, nblocks, edge_span)
    coef_tail, coef_head = endpoint_coefs(edge_dir, nblocks, edge_span)
    tail_match = tail_node.reshape(nblocks, edge_span)[:, :, None] == lax.iota(jnp.int32, bnodes)
    head_match = head_node.reshape(nblocks, edge_span)[:, :, None] == lax.iota(
        jnp.int32, 3 * bnodes
    )
    tail_hot = tail_match.astype(jnp.float32)
    head_hot = head_match.astype(jnp.float32)
    tail_part = jnp.einsum(
        "fske,ken->kfsn", coef_tail[:, None] * resid_blocks[None], tail_hot, precision=HIGHEST_PREC
    )
    head_part = jnp.einsum(
        "fske,ken->kfsn", coef_head[:, None] * resid_blocks[None], head_hot, precision=HIGHEST_PREC
    )
    padded = spread_heads(head_part, bnodes)
    nodal_sum = padded[2:] + tail_part
    rim_sum = shifted(padded[:2], "mesh", -1)
    nodal_sum = jnp.concatenate([nodal_sum[: nblocks - 2], nodal_sum[nblocks - 2 :] + rim_sum], 0)
    keep_mask = interior.reshape(nblocks, 1, 1, bnodes)
    restricted = (nodal_sum * keep_mask.astype(jnp.float32)).astype(jnp.bfloat16)
    restricted = restricted.reshape(nblocks * 4, src_dev, bnodes)
    grouped = lax.all_to_all(restricted, "src", split_axis=0, concat_axis=1, tiled=True)
    solved = block_sweep(grouped, block_inv, block_op)
    nodal = lax.all_to_all(solved, "src", split_axis=1, concat_axis=0, tiled=True)
    nodal = nodal.reshape(nblocks, 4, src_dev, bnodes) * keep_mask.astype(jnp.bfloat16)
    earlier = shifted(nodal[nblocks - 2 :], "mesh", 1)
    padded_corr = jnp.concatenate([earlier, nodal], 0)
    tail_low = tail_match.astype(jnp.bfloat16)
    head_low = head_match.astype(jnp.bfloat16).reshape(nblocks, edge_span, 3, bnodes)
    tail_vals = jnp.einsum(
        "kfsn,ken->fske", padded_corr[2:], tail_low, preferred_element_type=jnp.float32
    )
    windows = jnp.stack([padded_corr[offset : offset + nblocks] for offset in range(3)], 0)
    head_vals = jnp.einsum(
        "jkfsn,kejn->fske", windows, head_low, preferred_element_type=jnp.float32
    )
    summed = jnp.sum(coef_tail[:, None] * tail_vals + coef_head[:, None] * head_vals, axis=0)
    return summed.reshape(src_dev, edge_dev)


def solution(mesh):
    placed = (
        P("src", "mesh"),
        P("mesh"),
        P("src"),
        P("src"),
        P("mesh"),
        P(None, "mesh"),
        P("mesh"),
        P("mesh"),
        P(("mesh", "src"), None, None),
        P(("mesh", "src"), None, None),
    )
    return jax.shard_map(
        shards, mesh=mesh, in_specs=placed, out_specs=P("src", "mesh"), check_vma=False
    )
```

profile of v0, /device:TPU:1, one launch (start us, length us, event | category | flops | bytes accessed | tf_op | source)
XLA Modules:
  0.0 91.9 jit_solution(16786728489836537764)
XLA Ops:
  0.0 0.0 copy-start
  0.0 0.9 broadcast_multiply_fusion.2
  0.9 2.9 %multiply_subtract_fusion = f32[128,3072]{1,0:T(8,128)} fusion(f32[128,3072]{1,0:T(8,128)} %param.10, f32[3072]{0:T(1024)} %param.11, f32[128]{0:T(128)} %param.13, s32[3072]{0:T(1024)S(1)} %iota_add_fusion, s32[128]{0:T(128)} %param.12), kind=kLoop, calls=%fused_computation.34 | loop fusion | flops 1572864 | bytes 3171328 | tf_op jit(solution)/shard_map/sub | solution.py:59
  3.8 0.0 copy-start.2
  3.8 1.9 %copy.36 = f32[128,3072]{0,1:T(8,128)S(1)} copy(f32[128,3072]{1,0:T(8,128)} %multiply_subtract_fusion) | data formatting | bytes 3145728 | tf_op jit(solution)/shard_map/mul | solution.py:72
  5.7 0.0 copy-done.2
  5.7 11.7 %fusion.4 = f32[8,4,128,384]{3,2,1,0:T(8,128)S(1)} fusion(f32[128,8,384]{0,2,1:T(8,128)S(1)} %bitcast.66, f32[4,8,384]{2,0,1:T(4,128)S(1)} %get-tuple-element.11, s32[8,384]{1,0:T(8,128)S(1)} %eq.63), kind=kOutput, calls=%fused_computation.6 | convolution fusion | flops 7250509824 | bytes 7925760 | tf_op jit(solution)/shard_map/fske,ken->kfsn/dot_general | solution.py:71
  17.4 0.9 fusion.45
  18.3 0.1 pad_add_fusion.1
  18.3 0.0 copy-start.3
  18.3 1.9 %collective-permute-start = (f32[2,4,128,128]{3,2,1,0:T(8,128)S(1)}, f32[2,4,128,128]{3,2,1,0:T(8,128)S(1)}, u32[]{:S(2)}, u32[]{:S(2)}) collective-permute-start(f32[2,4,128,128]{3,2,1,0:T(8,128)S(1)} %pad_add_fusion.1), channel_id=1, source_target_pairs={{4,0},{8,4},{12,8},{16,12},{20,16},{24,20},{28,24},{5,1},{9,5},{13... | collective-permute-start | bytes 1572872 | tf_op jit(solution)/shard_map/ppermute | solution.py:14
  20.3 2.0 %pad_add_fusion = f32[10,4,128,128]{3,2,1,0:T(8,128)} fusion(f32[8,4,128,128]{3,2,1,0:T(8,128)S(1)} %get-tuple-element.6, f32[8,4,128,128]{3,2,1,0:T(8,128)S(1)} %get-tuple-element.7, f32[8,4,128,128]{3,2,1,0:T(8,128)S(1)} %get-tuple-element.5), kind=kLoop, calls=%fused_computation.22 | loop fusion | flops 1310720 | bytes 8912896 | tf_op jit(solution)/shard_map/add | solution.py:22
  22.3 0.0 copy-done.3
  22.3 9.9 %slice_add_fusion = f32[8,4,128,128]{3,2,1,0:T(8,128)S(1)} fusion(f32[10,4,128,128]{3,2,1,0:T(8,128)} %pad_add_fusion, f32[128,8,384]{0,2,1:T(8,128)S(1)} %bitcast.67, f32[4,8,384]{2,0,1:T(4,128)S(1)} %get-tuple-element.10, s32[8,384]{1,0:T(8,128)S(1)} %eq.56), kind=kOutput, calls=%fused_computation.26 | convolution fusion | flops 2418409472 | bytes 5828608 | tf_op jit(solution)/shard_map/fske,ken->kfsn/dot_general | solution.py:68
  32.2 0.0 copy-start.4
  32.2 0.1 slice.44
  32.3 0.6 copy-done.4
  32.9 0.0 collective-permute-done
  32.9 0.1 slice_add_fusion.1
  33.0 0.2 pad_maximum_fusion
  33.2 0.3 fusion.23
  33.5 19.0 %all_to_all.33 = bf16[32,128,128]{2,1,0:T(8,128)(2,1)S(1)} all-to-all(bf16[32,128,128]{2,1,0:T(8,128)(2,1)S(1)} %fusion.23), channel_id=1, replica_groups=mesh['mesh'=8,'src'=4] {'src'}, dimensions={0} | all-to-all | bytes 2097152 | tf_op jit(solution)/shard_map/all_to_all | solution.py:81
  52.4 0.1 copy.25
  52.5 0.0 copy-start.1
  52.5 0.0 copy-done
  52.5 1.0 %fusion.47 = f32[8,512,128]{2,1,0:T(8,128)S(1)} fusion(bf16[8,512,128]{2,1,0:T(8,128)(2,1)S(1)} %bitcast.70, f32[8,128,128]{2,1,0:T(8,128)S(1)} %copy-done), kind=kOutput, calls=%fused_computation.58 | convolution fusion | flops 805306368 | bytes 3670016 | tf_op jit(solution)/shard_map/ism,inm->isn/dot_general | solution.py:34
  53.6 0.0 copy-done.1
  53.6 2.0 %fusion.48 = f32[8,512,128]{2,1,0:T(8,128)S(1)} fusion(f32[8,512,128]{2,1,0:T(8,128)S(1)} %fusion.47, f32[8,128,128]{2,1,0:T(8,128)S(1)} %copy-done.1), kind=kOutput, calls=%fused_computation.59 | convolution fusion | flops 805306368 | bytes 4718592 | tf_op jit(solution)/shard_map/ism,inm->isn/dot_general | solution.py:35
  55.5 2.2 %add_convert_fusion = bf16[8,512,128]{2,1,0:T(8,128)(2,1)S(1)} fusion(f32[8,512,128]{2,1,0:T(8,128)S(1)} %fusion.47, f32[8,128,128]{2,1,0:T(8,128)S(1)} %copy-done, f32[8,512,128]{2,1,0:T(8,128)S(1)} %fusion.48, bf16[8,512,128]{2,1,0:T(8,128)(2,1)S(1)} %bitcast.71), kind=kOutput, calls=%fused_computation.30 | convolution fusion | flops 807403520 | bytes 6815744 | tf_op jit(solution)/shard_map/ism,inm->isn/dot_general | solution.py:36
  57.8 1.6 %copy.26 = bf16[8,512,128]{2,0,1:T(8,128)(2,1)} copy(bf16[8,512,128]{2,1,0:T(8,128)(2,1)S(1)} %add_convert_fusion) | data formatting | bytes 2097152 | tf_op jit(solution)/shard_map/convert_element_type | solution.py:37
  59.4 3.5 %all-to-all-start.1 = ((bf16[8,512,128]{2,0,1:T(8,128)(2,1)}), bf16[8,512,128]{2,0,1:T(8,128)(2,1)S(1)}, u32[]{:S(2)}, u32[]{:S(2)}) async-start(bf16[8,512,128]{2,0,1:T(8,128)(2,1)} %copy.26), calls=%async_computation.1 | async-start | bytes 2097152 | tf_op jit(solution)/shard_map/all_to_all | solution.py:83
  63.0 13.1 %all-to-all-done.1 = bf16[8,512,128]{2,0,1:T(8,128)(2,1)S(1)} async-done(((bf16[8,512,128]{2,0,1:T(8,128)(2,1)}), bf16[8,512,128]{2,0,1:T(8,128)(2,1)S(1)}, u32[]{:S(2)}, u32[]{:S(2)}) %all-to-all-start.1) | async-done | bytes 1048608 | tf_op jit(solution)/shard_map/all_to_all | solution.py:83
  76.1 0.2 copy.27
  76.3 0.1 broadcast_multiply_fusion.1
  76.4 1.7 %fusion.30 = f32[8,384,4,128]{3,1,2,0:T(8,128)S(1)} fusion(bf16[8,4,128,128]{3,2,1,0:T(8,128)(2,1)S(1)} %broadcast_multiply_fusion.1, s32[8,384]{1,0:T(8,128)S(1)} %eq.56), kind=kOutput, calls=%fused_computation.37 | convolution fusion | flops 403046400 | bytes 7352320 | tf_op jit(solution)/shard_map/kfsn,ken->fske/dot_general | solution.py:89
  78.2 3.9 %collective-permute-start.1 = (bf16[2,4,128,128]{3,2,1,0:T(8,128)(2,1)S(1)}, bf16[2,4,128,128]{3,2,1,0:T(8,128)(2,1)S(1)}, u32[]{:S(2)}, u32[]{:S(2)}) collective-permute-start(bf16[2,4,128,128]{3,2,1,0:T(8,128)(2,1)S(1)} %slice.46), channel_id=1, source_target_pairs={{0,4},{4,8},{8,12},{12,16},{16,20},{20,24},{24,28},{1,5},{5,9},{9,... | collective-permute-start | bytes 786440 | tf_op jit(solution)/shard_map/ppermute | solution.py:14
  82.1 0.1 broadcast_multiply_fusion
  82.2 3.2 %collective-permute-done.1 = bf16[2,4,128,128]{3,2,1,0:T(8,128)(2,1)S(1)} collective-permute-done((bf16[2,4,128,128]{3,2,1,0:T(8,128)(2,1)S(1)}, bf16[2,4,128,128]{3,2,1,0:T(8,128)(2,1)S(1)}, u32[]{:S(2)}, u32[]{:S(2)}) %collective-permute-start.1) | collective-permute-done | bytes 262176 | tf_op jit(solution)/shard_map/ppermute | solution.py:14
  85.4 0.1 fusion.40
  85.5 4.8 %fusion.1 = f32[128,8,384]{0,2,1:T(8,128)S(1)} fusion(f32[8,384,4,128]{3,1,2,0:T(8,128)S(1)} %fusion.30, f32[4,8,384]{2,0,1:T(4,128)S(1)} %get-tuple-element.11, f32[4,8,384]{2,0,1:T(4,128)S(1)} %get-tuple-element.10, bf16[1,8,4,128,128]{4,3,0,2,1:T(8,128)(2,1)S(1)} %broadcast_multiply_fusion, bf16[1,8,4,128,128]{4,3,0,2,1:T(8,128)(2,1)S(1)} %get-tuple-element.9, ...), kind=kOutput, calls=%fused_computation.2 | convolution fusion | flops 1224474624 | bytes 11122176 | tf_op jit(solution)/shard_map/jkfsn,kejn->fske/dot_general | solution.py:93
  90.3 1.6 %copy.29 = f32[128,3072]{1,0:T(8,128)} copy(f32[128,3072]{0,1:T(8,128)S(1)} %bitcast.74) | data formatting | bytes 3145728 | tf_op jit(solution)/shard_map/reshape | solution.py:97
  (8 shorter events, 0.1 us)
Async XLA Ops:
  0.0 52.5 %copy-start = (f32[8,128,128]{2,1,0:T(8,128)S(1)}, f32[8,128,128]{2,1,0:T(8,128)}, u32[]{:S(2)}) copy-start(f32[8,128,128]{2,1,0:T(8,128)} %param.18) | copy-start | bytes 1572868
  3.8 1.9 %copy-start.2 = (s32[3072]{0:T(1024)S(1)}, s32[3072]{0:T(1024)}, u32[]{:S(2)}) copy-start(s32[3072]{0:T(1024)} %param.17) | copy-start | bytes 36868
  18.3 4.0 %copy-start.3 = (s32[3072]{0:T(1024)S(1)}, s32[3072]{0:T(1024)}, u32[]{:S(2)}) copy-start(s32[3072]{0:T(1024)} %param.16) | copy-start | bytes 36868
  18.3 14.6 %collective-permute-start = (f32[2,4,128,128]{3,2,1,0:T(8,128)S(1)}, f32[2,4,128,128]{3,2,1,0:T(8,128)S(1)}, u32[]{:S(2)}, u32[]{:S(2)}) collective-permute-start(f32[2,4,128,128]{3,2,1,0:T(8,128)S(1)} %pad_add_fusion.1), channel_id=1, source_target_pairs={{4,0},{8,4},{12,8},{16,12},{20,16},{24,20},{28,24},{5,1},{9,5},{13... | collective-permute-start | bytes 1572872 | tf_op jit(solution)/shard_map/ppermute | solution.py:14
  32.2 0.7 copy-start.4
  52.5 1.0 %copy-start.1 = (f32[8,128,128]{2,1,0:T(8,128)S(1)}, f32[8,128,128]{2,1,0:T(8,128)}, u32[]{:S(2)}) copy-start(f32[8,128,128]{2,1,0:T(8,128)} %param.19) | copy-start | bytes 1572868
  59.4 16.6 %all-to-all-start.1 = ((bf16[8,512,128]{2,0,1:T(8,128)(2,1)}), bf16[8,512,128]{2,0,1:T(8,128)(2,1)S(1)}, u32[]{:S(2)}, u32[]{:S(2)}) async-start(bf16[8,512,128]{2,0,1:T(8,128)(2,1)} %copy.26), calls=%async_computation.1 | async-start | bytes 2097152 | tf_op jit(solution)/shard_map/all_to_all | solution.py:83
  78.2 7.2 %collective-permute-start.1 = (bf16[2,4,128,128]{3,2,1,0:T(8,128)(2,1)S(1)}, bf16[2,4,128,128]{3,2,1,0:T(8,128)(2,1)S(1)}, u32[]{:S(2)}, u32[]{:S(2)}) collective-permute-start(bf16[2,4,128,128]{3,2,1,0:T(8,128)(2,1)S(1)} %slice.46), channel_id=1, source_target_pairs={{0,4},{4,8},{8,12},{12,16},{16,20},{20,24},{24,28},{1,5},{5,9},{9,... | collective-permute-start | bytes 786440 | tf_op jit(solution)/shard_map/ppermute | solution.py:14
where the time goes:
time: 92.4 us; the launch traced here: 91.9 us
  matrix products  33.3 us (36%)
  blocking collectives  19 us (21%)
  waiting for transfers between devices  16.3 us (18%)
  starting transfers between devices  9.33 us (10%)
  local copies, waits for them, and re-layouts  7.08 us (8%)
  other arithmetic  6.64 us (7%)
    all_to_all x1, blocking collectives, shards(): lax.all_to_all(restricted, 'src', split_axis=0, concat_axis=1, tiled=True)  19 us
    all_to_all x1, waiting for transfers between devices, shards(): lax.all_to_all(solved, 'src', split_axis=1, concat_axis=0, tiled=True)  13.1 us
    dot_general x1, matrix products, shards(): jnp.einsum('fske,ken->kfsn', coef_head[:, None] * resid_blocks[None], hea...  11.7 us
    dot_general x1, matrix products, shards(): jnp.einsum('fske,ken->kfsn', coef_tail[:, None] * resid_blocks[None], tai...  9.91 us
    ppermute x2, starting transfers between devices, shifted(): return lax.ppermute(x, axis, pairs)  5.81 us
    dot_general x1, matrix products, shards(): jnp.einsum('jkfsn,kejn->fske', windows, head_low, preferred_element_type=...  4.77 us
    all_to_all x1, starting transfers between devices, shards(): lax.all_to_all(solved, 'src', split_axis=1, concat_axis=0, tiled=True)  3.52 us
    ppermute x2, waiting for transfers between devices, shifted(): return lax.ppermute(x, axis, pairs)  3.22 us
  transfers between devices with their start and end apart: 3, of which 2 were waited for; matrix products, arithmetic and copies ran while one was open for 13% of the time, Pallas kernels for 0%

commit v1 on v0

--- a/solution.py
+++ b/solution.py
@@ -78,7 +78,9 @@
     keep_mask = interior.reshape(nblocks, 1, 1, bnodes)
     restricted = (nodal_sum * keep_mask.astype(jnp.float32)).astype(jnp.bfloat16)
     restricted = restricted.reshape(nblocks * 4, src_dev, bnodes)
-    grouped = lax.all_to_all(restricted, "src", split_axis=0, concat_axis=1, tiled=True)
+    parts = jnp.split(restricted, lax.axis_size("src"), axis=0)
+    got = lax.all_to_all(jnp.stack(parts), "src", 0, 0)
+    grouped = jnp.concatenate(got, axis=1)
     solved = block_sweep(grouped, block_inv, block_op)
     nodal = lax.all_to_all(solved, "src", split_axis=1, concat_axis=0, tiled=True)
     nodal = nodal.reshape(nblocks, 4, src_dev, bnodes) * keep_mask.astype(jnp.bfloat16)

time: 92.4 us -> 92.4 us (level)
  no operation moved by 1% of the time
where the time goes in v1:
time: 92.4 us; the launch traced here: 91.9 us
  matrix products  33.3 us (36%)
  blocking collectives  19 us (21%)
  waiting for transfers between devices  16.3 us (18%)
  starting transfers between devices  9.33 us (10%)
  local copies, waits for them, and re-layouts  7.15 us (8%)
  other arithmetic  6.56 us (7%)
    all_to_all x1, blocking collectives, shards(): got = lax.all_to_all(jnp.stack(parts), 'src', 0, 0)  19 us
    all_to_all x1, waiting for transfers between devices, shards(): lax.all_to_all(solved, 'src', split_axis=1, concat_axis=0, tiled=True)  13.1 us
    dot_general x1, matrix products, shards(): jnp.einsum('fske,ken->kfsn', coef_head[:, None] * resid_blocks[None], hea...  11.7 us
    dot_general x1, matrix products, shards(): jnp.einsum('fske,ken->kfsn', coef_tail[:, None] * resid_blocks[None], tai...  9.9 us
    ppermute x2, starting transfers between devices, shifted(): return lax.ppermute(x, axis, pairs)  5.81 us
    dot_general x1, matrix products, shards(): jnp.einsum('jkfsn,kejn->fske', windows, head_low, preferred_element_type=...  4.77 us
    all_to_all x1, starting transfers between devices, shards(): lax.all_to_all(solved, 'src', split_axis=1, concat_axis=0, tiled=True)  3.52 us
    ppermute x2, waiting for transfers between devices, shifted(): return lax.ppermute(x, axis, pairs)  3.22 us
  transfers between devices with their start and end apart: 3, of which 2 were waited for; matrix products, arithmetic and copies ran while one was open for 13% of the time, Pallas kernels for 0%

profile of v1, /device:TPU:1, one launch (start us, length us, event | category | flops | bytes accessed | tf_op | source)
XLA Modules:
  0.0 91.9 jit_solution(1721062712600898315)
XLA Ops:
  0.0 0.0 copy-start
  0.0 0.9 broadcast_multiply_fusion.2
  0.9 2.9 %multiply_subtract_fusion = f32[128,3072]{1,0:T(8,128)} fusion(f32[128,3072]{1,0:T(8,128)} %param.10, f32[3072]{0:T(1024)} %param.11, f32[128]{0:T(128)} %param.13, s32[3072]{0:T(1024)S(1)} %iota_add_fusion, s32[128]{0:T(128)} %param.12), kind=kLoop, calls=%fused_computation.33 | loop fusion | flops 1572864 | bytes 3171328 | tf_op jit(solution)/shard_map/sub | solution.py:59
  3.8 0.0 copy-start.2
  3.8 1.9 %copy.36 = f32[128,3072]{0,1:T(8,128)S(1)} copy(f32[128,3072]{1,0:T(8,128)} %multiply_subtract_fusion) | data formatting | bytes 3145728 | tf_op jit(solution)/shard_map/mul | solution.py:72
  5.7 0.0 copy-done.2
  5.7 11.7 %fusion.4 = f32[8,4,128,384]{3,2,1,0:T(8,128)S(1)} fusion(f32[128,8,384]{0,2,1:T(8,128)S(1)} %bitcast.63, f32[4,8,384]{2,0,1:T(4,128)S(1)} %get-tuple-element.15, s32[8,384]{1,0:T(8,128)S(1)} %eq.63), kind=kOutput, calls=%fused_computation.6 | convolution fusion | flops 7250509824 | bytes 7925760 | tf_op jit(solution)/shard_map/fske,ken->kfsn/dot_general | solution.py:71
  17.4 0.9 fusion.45
  18.3 0.1 pad_add_fusion.1
  18.3 0.0 copy-start.3
  18.3 1.9 %collective-permute-start = (f32[2,4,128,128]{3,2,1,0:T(8,128)S(1)}, f32[2,4,128,128]{3,2,1,0:T(8,128)S(1)}, u32[]{:S(2)}, u32[]{:S(2)}) collective-permute-start(f32[2,4,128,128]{3,2,1,0:T(8,128)S(1)} %pad_add_fusion.1), channel_id=1, source_target_pairs={{4,0},{8,4},{12,8},{16,12},{20,16},{24,20},{28,24},{5,1},{9,5},{13... | collective-permute-start | bytes 1572872 | tf_op jit(solution)/shard_map/ppermute | solution.py:14
  20.3 2.0 %pad_add_fusion = f32[10,4,128,128]{3,2,1,0:T(8,128)} fusion(f32[8,4,128,128]{3,2,1,0:T(8,128)S(1)} %get-tuple-element.6, f32[8,4,128,128]{3,2,1,0:T(8,128)S(1)} %get-tuple-element.7, f32[8,4,128,128]{3,2,1,0:T(8,128)S(1)} %get-tuple-element.5), kind=kLoop, calls=%fused_computation.22 | loop fusion | flops 1310720 | bytes 8912896 | tf_op jit(solution)/shard_map/add | solution.py:22
  22.3 0.0 copy-done.3
  22.3 9.9 %slice_add_fusion = f32[8,4,128,128]{3,2,1,0:T(8,128)S(1)} fusion(f32[10,4,128,128]{3,2,1,0:T(8,128)} %pad_add_fusion, f32[128,8,384]{0,2,1:T(8,128)S(1)} %bitcast.64, f32[4,8,384]{2,0,1:T(4,128)S(1)} %get-tuple-element.14, s32[8,384]{1,0:T(8,128)S(1)} %eq.56), kind=kOutput, calls=%fused_computation.26 | convolution fusion | flops 2418409472 | bytes 5828608 | tf_op jit(solution)/shard_map/fske,ken->kfsn/dot_general | solution.py:68
  32.2 0.0 copy-start.4
  32.2 0.1 slice.48
  32.3 0.6 copy-done.4
  32.9 0.0 collective-permute-done
  32.9 0.1 slice_add_fusion.1
  33.0 0.3 fusion.23
  33.2 0.1 fusion.46
  33.3 0.1 pad_maximum_fusion.1
  33.5 19.0 %all_to_all.20 = bf16[4,8,128,128]{3,2,1,0:T(8,128)(2,1)S(1)} all-to-all(bf16[4,8,128,128]{3,2,1,0:T(8,128)(2,1)S(1)} %pad_maximum_fusion.1), channel_id=1, replica_groups=mesh['mesh'=8,'src'=4] {'src'}, dimensions={0} | all-to-all | bytes 2097152 | tf_op jit(solution)/shard_map/all_to_all | solution.py:82
  52.4 0.1 copy.25
  52.5 0.0 copy-start.1
  52.5 0.0 copy-done
  52.5 1.0 %fusion.48 = f32[8,512,128]{2,1,0:T(8,128)S(1)} fusion(bf16[8,512,128]{2,1,0:T(8,128)(2,1)S(1)} %bitcast.67, f32[8,128,128]{2,1,0:T(8,128)S(1)} %copy-done), kind=kOutput, calls=%fused_computation.59 | convolution fusion | flops 805306368 | bytes 3670016 | tf_op jit(solution)/shard_map/ism,inm->isn/dot_general | solution.py:34
  53.5 0.0 copy-done.1
  53.6 2.0 %fusion.49 = f32[8,512,128]{2,1,0:T(8,128)S(1)} fusion(f32[8,512,128]{2,1,0:T(8,128)S(1)} %fusion.48, f32[8,128,128]{2,1,0:T(8,128)S(1)} %copy-done.1), kind=kOutput, calls=%fused_computation.60 | convolution fusion | flops 805306368 | bytes 4718592 | tf_op jit(solution)/shard_map/ism,inm->isn/dot_general | solution.py:35
  55.5 2.2 %add_convert_fusion = bf16[8,512,128]{2,1,0:T(8,128)(2,1)S(1)} fusion(f32[8,512,128]{2,1,0:T(8,128)S(1)} %fusion.48, f32[8,128,128]{2,1,0:T(8,128)S(1)} %copy-done, f32[8,512,128]{2,1,0:T(8,128)S(1)} %fusion.49, bf16[8,512,128]{2,1,0:T(8,128)(2,1)S(1)} %bitcast.68), kind=kOutput, calls=%fused_computation.29 | convolution fusion | flops 807403520 | bytes 6815744 | tf_op jit(solution)/shard_map/ism,inm->isn/dot_general | solution.py:36
  57.8 1.6 %copy.26 = bf16[8,512,128]{2,0,1:T(8,128)(2,1)} copy(bf16[8,512,128]{2,1,0:T(8,128)(2,1)S(1)} %add_convert_fusion) | data formatting | bytes 2097152 | tf_op jit(solution)/shard_map/convert_element_type | solution.py:37
  59.4 3.5 %all-to-all-start.1 = ((bf16[8,512,128]{2,0,1:T(8,128)(2,1)}), bf16[8,512,128]{2,0,1:T(8,128)(2,1)S(1)}, u32[]{:S(2)}, u32[]{:S(2)}) async-start(bf16[8,512,128]{2,0,1:T(8,128)(2,1)} %copy.26), calls=%async_computation.1 | async-start | bytes 2097152 | tf_op jit(solution)/shard_map/all_to_all | solution.py:85
  63.0 13.1 %all-to-all-done.1 = bf16[8,512,128]{2,0,1:T(8,128)(2,1)S(1)} async-done(((bf16[8,512,128]{2,0,1:T(8,128)(2,1)}), bf16[8,512,128]{2,0,1:T(8,128)(2,1)S(1)}, u32[]{:S(2)}, u32[]{:S(2)}) %all-to-all-start.1) | async-done | bytes 1048608 | tf_op jit(solution)/shard_map/all_to_all | solution.py:85
  76.1 0.2 copy.27
  76.3 0.1 broadcast_multiply_fusion.1
  76.4 1.7 %fusion.30 = f32[8,384,4,128]{3,1,2,0:T(8,128)S(1)} fusion(bf16[8,4,128,128]{3,2,1,0:T(8,128)(2,1)S(1)} %broadcast_multiply_fusion.1, s32[8,384]{1,0:T(8,128)S(1)} %eq.56), kind=kOutput, calls=%fused_computation.36 | convolution fusion | flops 403046400 | bytes 7352320 | tf_op jit(solution)/shard_map/kfsn,ken->fske/dot_general | solution.py:91
  78.2 3.9 %collective-permute-start.1 = (bf16[2,4,128,128]{3,2,1,0:T(8,128)(2,1)S(1)}, bf16[2,4,128,128]{3,2,1,0:T(8,128)(2,1)S(1)}, u32[]{:S(2)}, u32[]{:S(2)}) collective-permute-start(bf16[2,4,128,128]{3,2,1,0:T(8,128)(2,1)S(1)} %slice.50), channel_id=1, source_target_pairs={{0,4},{4,8},{8,12},{12,16},{16,20},{20,24},{24,28},{1,5},{5,9},{9,... | collective-permute-start | bytes 786440 | tf_op jit(solution)/shard_map/ppermute | solution.py:14
  82.1 0.1 broadcast_multiply_fusion
  82.2 3.2 %collective-permute-done.1 = bf16[2,4,128,128]{3,2,1,0:T(8,128)(2,1)S(1)} collective-permute-done((bf16[2,4,128,128]{3,2,1,0:T(8,128)(2,1)S(1)}, bf16[2,4,128,128]{3,2,1,0:T(8,128)(2,1)S(1)}, u32[]{:S(2)}, u32[]{:S(2)}) %collective-permute-start.1) | collective-permute-done | bytes 262176 | tf_op jit(solution)/shard_map/ppermute | solution.py:14
  85.4 0.1 fusion.40
  85.5 4.8 %fusion.1 = f32[128,8,384]{0,2,1:T(8,128)S(1)} fusion(f32[8,384,4,128]{3,1,2,0:T(8,128)S(1)} %fusion.30, f32[4,8,384]{2,0,1:T(4,128)S(1)} %get-tuple-element.15, f32[4,8,384]{2,0,1:T(4,128)S(1)} %get-tuple-element.14, bf16[1,8,4,128,128]{4,3,0,2,1:T(8,128)(2,1)S(1)} %broadcast_multiply_fusion, bf16[1,8,4,128,128]{4,3,0,2,1:T(8,128)(2,1)S(1)} %get-tuple-element.9, ...), kind=kOutput, calls=%fused_computation.2 | convolution fusion | flops 1224474624 | bytes 11122176 | tf_op jit(solution)/shard_map/jkfsn,kejn->fske/dot_general | solution.py:95
  90.3 1.6 %copy.29 = f32[128,3072]{1,0:T(8,128)} copy(f32[128,3072]{0,1:T(8,128)S(1)} %bitcast.71) | data formatting | bytes 3145728 | tf_op jit(solution)/shard_map/reshape | solution.py:99
  (7 shorter events, 0.1 us)
Async XLA Ops:
  0.0 52.5 %copy-start = (f32[8,128,128]{2,1,0:T(8,128)S(1)}, f32[8,128,128]{2,1,0:T(8,128)}, u32[]{:S(2)}) copy-start(f32[8,128,128]{2,1,0:T(8,128)} %param.18) | copy-start | bytes 1572868
  3.8 1.9 %copy-start.2 = (s32[3072]{0:T(1024)S(1)}, s32[3072]{0:T(1024)}, u32[]{:S(2)}) copy-start(s32[3072]{0:T(1024)} %param.17) | copy-start | bytes 36868
  18.3 4.0 %copy-start.3 = (s32[3072]{0:T(1024)S(1)}, s32[3072]{0:T(1024)}, u32[]{:S(2)}) copy-start(s32[3072]{0:T(1024)} %param.16) | copy-start | bytes 36868
  18.3 14.6 %collective-permute-start = (f32[2,4,128,128]{3,2,1,0:T(8,128)S(1)}, f32[2,4,128,128]{3,2,1,0:T(8,128)S(1)}, u32[]{:S(2)}, u32[]{:S(2)}) collective-permute-start(f32[2,4,128,128]{3,2,1,0:T(8,128)S(1)} %pad_add_fusion.1), channel_id=1, source_target_pairs={{4,0},{8,4},{12,8},{16,12},{20,16},{24,20},{28,24},{5,1},{9,5},{13... | collective-permute-start | bytes 1572872 | tf_op jit(solution)/shard_map/ppermute | solution.py:14
  32.2 0.7 copy-start.4
  52.5 1.0 %copy-start.1 = (f32[8,128,128]{2,1,0:T(8,128)S(1)}, f32[8,128,128]{2,1,0:T(8,128)}, u32[]{:S(2)}) copy-start(f32[8,128,128]{2,1,0:T(8,128)} %param.19) | copy-start | bytes 1572868
  59.4 16.7 %all-to-all-start.1 = ((bf16[8,512,128]{2,0,1:T(8,128)(2,1)}), bf16[8,512,128]{2,0,1:T(8,128)(2,1)S(1)}, u32[]{:S(2)}, u32[]{:S(2)}) async-start(bf16[8,512,128]{2,0,1:T(8,128)(2,1)} %copy.26), calls=%async_computation.1 | async-start | bytes 2097152 | tf_op jit(solution)/shard_map/all_to_all | solution.py:85
  78.2 7.2 %collective-permute-start.1 = (bf16[2,4,128,128]{3,2,1,0:T(8,128)(2,1)S(1)}, bf16[2,4,128,128]{3,2,1,0:T(8,128)(2,1)S(1)}, u32[]{:S(2)}, u32[]{:S(2)}) collective-permute-start(bf16[2,4,128,128]{3,2,1,0:T(8,128)(2,1)S(1)} %slice.50), channel_id=1, source_target_pairs={{0,4},{4,8},{8,12},{12,16},{16,20},{20,24},{24,28},{1,5},{5,9},{9,... | collective-permute-start | bytes 786440 | tf_op jit(solution)/shard_map/ppermute | solution.py:14
